TPU v7x, 32 devices: a whole 2x2x4 slice. The times are simulated.
32 devices in a mesh: row: 8 (over z, y), col: 4 (over x, core).
Axes of the slice: x: 2, y: 2, z: 4, core: 2. Of those that a mesh axis runs over, the one named last changes fastest.
Arguments:
- image: bfloat16 [2048, 512], P(('row', 'col')), may hold values from -2 to 2
- text: bfloat16 [2048, 512], P(('row', 'col')), may hold values from -3 to 3
- logit_scale: float32 [1], replicated, may hold values from 10 to 100
Outputs:
- loss: float32 [1], replicated
- grad_image: float32 [2048, 512], P(('row', 'col'))
- grad_text: float32 [2048, 512], P(('row', 'col'))
All inputs are finite; a program needn't handle non-finite values.
Results may differ from a plain program's by a relative error of at most 0.0095.
Values may be sent and summed in bfloat16 or wider, within the bound.
No kernel may reach another device: no remote copies, remote signals or barrier semaphores. Data moves between devices by JAX's collectives and lax.ppermute only.
A program may use at most 64 MiB of HBM per device.

v0:
```python
import jax
import jax.numpy as jnp
from jax import lax
from jax.sharding import PartitionSpec as P


def normalize(embedding):
    values = embedding.astype(jnp.float32)
    length = jnp.sqrt(jnp.sum(values * values, axis=1, keepdims=True) + 1e-06)
    return (values / length, length)


def unnormalize(unit_rows, length, gradient):
    return (gradient - unit_rows * jnp.sum(unit_rows * gradient, axis=1, keepdims=True)) / length


def on_device(image, text, logit_scale):
    sharpness = logit_scale[0]
    unit_image, image_len = normalize(image)
    unit_text, text_len = normalize(text)
    img_own = unit_image.astype(jnp.bfloat16)
    txt_own = unit_text.astype(jnp.bfloat16)
    img_tile = lax.all_gather(img_own, "col", axis=0, tiled=True)
    txt_tile = lax.all_gather(txt_own, "row", axis=0, tiled=True)
    columns = txt_tile.shape[0]
    block_cols = min(512, columns)
    block_count = columns // block_cols
    txt_blocks = txt_tile.reshape(block_count, block_cols, txt_tile.shape[1])

    def scores(txt_block):
        return sharpness * jnp.einsum(
            "re,ce->rc", img_tile, txt_block, preferred_element_type=jnp.float32
        )

    lowest = jnp.full((img_tile.shape[0],), -1e30, jnp.float32)

    def peaks(running, txt_block):
        logits = scores(txt_block)
        return (jnp.maximum(running, jnp.max(logits, axis=1)), jnp.max(logits, axis=0))

    row_peak, col_peak = lax.scan(peaks, lowest, txt_blocks)
    row_peak = lax.pmax(row_peak, "col")
    col_peak = lax.pmax(col_peak.reshape(-1), "row")

    def sums(running, inputs):
        txt_block, peak_cols = inputs
        logits = scores(txt_block)
        running = running + jnp.sum(jnp.exp(logits - row_peak[:, None]), axis=1)
        return (running, jnp.sum(jnp.exp(logits - peak_cols[None, :]), axis=0))

    row_sum, col_sum = lax.scan(
        sums, jnp.zeros_like(lowest), (txt_blocks, col_peak.reshape(block_count, block_cols))
    )
    row_sum = lax.psum(row_sum, "col")
    col_sum = lax.psum(col_sum.reshape(-1), "row")
    row_lse = row_peak + jnp.log(row_sum)
    col_lse = col_peak + jnp.log(col_sum)
    own_rows = image.shape[0]
    row_mine = lax.dynamic_slice_in_dim(row_lse, lax.axis_index("col") * own_rows, own_rows)
    col_mine = lax.dynamic_slice_in_dim(col_lse, lax.axis_index("row") * own_rows, own_rows)
    img_wide = img_own.astype(jnp.float32)
    txt_wide = txt_own.astype(jnp.float32)
    positive = sharpness * jnp.sum(img_wide * txt_wide, axis=1)
    partial_value = jnp.sum(row_mine - positive) + jnp.sum(col_mine - positive)
    overall = lax.psum(partial_value, ("row", "col"))
    batch_size = own_rows * lax.axis_size("row") * lax.axis_size("col")
    loss = (overall / (2 * batch_size)).reshape(1)

    def weights_of(txt_block, lse_cols):
        logits = scores(txt_block)
        return (
            0.5 * (jnp.exp(logits - row_lse[:, None]) + jnp.exp(logits - lse_cols[None, :]))
        ).astype(jnp.bfloat16)

    start_grad = jnp.zeros((img_tile.shape[0], img_tile.shape[1]), jnp.float32)
    lse_blocks = col_lse.reshape(block_count, block_cols)

    def backward(running, inputs):
        txt_block, lse_cols = inputs
        weights = weights_of(txt_block, lse_cols)
        running = running + sharpness * jnp.dot(
            weights, txt_block, preferred_element_type=jnp.float32
        )
        return (
            running,
            sharpness
            * jnp.einsum("rc,re->ce", weights, img_tile, preferred_element_type=jnp.float32),
        )

    img_terms, txt_terms = lax.scan(backward, start_grad, (txt_blocks, lse_blocks))
    txt_grad = lax.psum_scatter(
        txt_terms.reshape(columns, img_tile.shape[1]), "row", scatter_dimension=0, tiled=True
    )
    img_grad = lax.psum_scatter(img_terms, "col", scatter_dimension=0, tiled=True)
    img_grad = img_grad - sharpness * txt_wide
    txt_grad = txt_grad - sharpness * img_wide
    return (
        loss,
        unnormalize(unit_image, image_len, img_grad),
        unnormalize(unit_text, text_len, txt_grad),
    )


def solution(mesh):
    placed = (P(("row", "col"), None), P(("row", "col"), None), P())
    return jax.shard_map(
        on_device,
        mesh=mesh,
        in_specs=placed,
        out_specs=(P(), P(("row", "col"), None), P(("row", "col"), None)),
        check_vma=False,
    )
```

profile of v0, /device:TPU:0, one launch (start us, length us, event | category | flops | bytes accessed | tf_op | source)
XLA Modules:
  0.0 241.8 jit_solution(7064855430679958634)
XLA Ops:
  7.2 0.0 copy-start.1
  7.2 0.0 reduce-scatter.3.cloned.1.call-start
  7.9 1.0 fusion.1
  8.8 0.0 copy-done.1
  8.8 0.1 fusion.6
  8.9 0.0 copy-start
  9.0 33.2 %all_gather.7 = bf16[512,512]{1,0:T(8,128)(2,1)S(1)} all-gather(bf16[64,512]{1,0:T(8,128)(2,1)S(1)} %fusion.6), channel_id=1, replica_groups=mesh['row'=8,'col'=4] {'row'}, dimensions={0}, use_global_device_ids=true | all-gather | bytes 589824 | tf_op jit(solution)/shard_map/all_gather | solution.py:24
  42.1 0.0 copy-done
  42.1 0.1 fusion
  42.2 0.1 fusion.5
  42.3 5.8 %all_gather.6 = bf16[256,512]{1,0:T(8,128)(2,1)S(1)} all-gather(bf16[64,512]{1,0:T(8,128)(2,1)S(1)} %fusion.5), channel_id=1, replica_groups=mesh['row'=8,'col'=4] {'col'}, dimensions={0}, use_global_device_ids=true | all-gather | bytes 327680 | tf_op jit(solution)/shard_map/all_gather | solution.py:23
  48.1 0.4 fusion.7
  48.6 7.1 %pmax.14 = f32[256]{0:T(256)S(1)} all-reduce(f32[256]{0:T(256)S(1)} %broadcast_maximum_fusion), channel_id=1, replica_groups=mesh['row'=8,'col'=4] {'col'}, use_global_device_ids=true, to_apply=%region_3.0 | all-reduce | flops 256 | bytes 2048 | tf_op jit(solution)/shard_map/pmax | solution.py:42
  55.6 21.5 %pmax.15 = f32[512]{0:T(512)S(1)} all-reduce(f32[512]{0:T(512)S(1)} %get-tuple-element.47), channel_id=1, replica_groups=mesh['row'=8,'col'=4] {'row'}, use_global_device_ids=true, to_apply=%region_9.10 | all-reduce | flops 512 | bytes 4096 | tf_op jit(solution)/shard_map/pmax | solution.py:43
  77.2 0.2 exponential_reduce_fusion
  77.4 5.9 %psum.21 = f32[256]{0:T(256)S(1)} all-reduce(f32[256]{0:T(256)S(1)} %get-tuple-element.46), channel_id=1, replica_groups=mesh['row'=8,'col'=4] {'col'}, use_global_device_ids=true, to_apply=%region_5.6 | all-reduce | flops 256 | bytes 2048 | tf_op jit(solution)/shard_map/psum | solution.py:54
  83.3 17.1 %psum.22 = f32[512]{0:T(512)S(1)} all-reduce(f32[512]{0:T(512)S(1)} %get-tuple-element.45), channel_id=1, replica_groups=mesh['row'=8,'col'=4] {'row'}, use_global_device_ids=true, to_apply=%region_11.12 | all-reduce | flops 512 | bytes 4096 | tf_op jit(solution)/shard_map/psum | solution.py:55
  100.4 1.2 convolution_multiply_fusion.1
  101.7 0.0 reduce-scatter.3.cloned.1.call-update
  101.7 0.0 reduce-scatter.5.cloned.1.call-start
  101.7 1.5 convolution_multiply_fusion
  103.2 0.0 reduce-scatter.5.cloned.1.call-update
  103.2 18.0 %reduce-scatter.3.cloned.1.call-done = f32[64,512]{1,0:T(8,128)} async-done(((f32[256,512]{1,0:T(8,128)}), f32[64,512]{1,0:T(8,128)}) %reduce-scatter.3.cloned.1.call-update) | async-done | bytes 131088 | tf_op jit(solution)/shard_map/reduce_scatter | solution.py:94
  121.2 68.0 %reduce-scatter.5.cloned.1.call-done = f32[64,512]{1,0:T(8,128)} async-done(((f32[512,512]{1,0:T(8,128)}), f32[64,512]{1,0:T(8,128)}) %reduce-scatter.5.cloned.1.call-update) | async-done | bytes 131088 | tf_op jit(solution)/shard_map/reduce_scatter | solution.py:91
  189.2 0.0 copy-start.2
  189.2 0.0 copy-start.3
  189.2 1.3 multiply_reduce_fusion
  190.5 0.7 subtract_reduce_fusion
  192.5 39.9 %psum.23 = f32[]{:T(128)} all-reduce(f32[]{:T(128)S(6)} %add.61), channel_id=1, replica_groups=mesh['row'=8,'col'=4] {'row','col'}, use_global_device_ids=true, to_apply=%region_13.14 | all-reduce | flops 1 | bytes 8 | tf_op jit(solution)/shard_map/psum | solution.py:65
  233.0 0.0 copy-done.2
  233.0 0.0 copy-done.3
  233.0 0.8 subtract_divide_fusion
  (5 shorter events, 0.0 us)
Async XLA Ops:
  7.2 1.7 copy-start.1
  7.2 114.1 %reduce-scatter.3.cloned.1.call-start = ((), (), s32[]{:S(2)}) async-start(), calls=%async_computation.2 | async-start | bytes 655360 | tf_op jit(solution)/shard_map/reduce_scatter | solution.py:94
  8.9 33.2 %copy-start = (bf16[64,512]{1,0:T(8,128)(2,1)S(1)}, bf16[64,512]{1,0:T(8,128)(2,1)}, u32[]{:S(2)}) copy-start(bf16[64,512]{1,0:T(8,128)(2,1)} %param.3) | copy-start | bytes 196612
  101.7 87.6 %reduce-scatter.5.cloned.1.call-start = ((), (), s32[]{:S(2)}) async-start(), calls=%async_computation.3 | async-start | bytes 1179648 | tf_op jit(solution)/shard_map/reduce_scatter | solution.py:91
  189.2 43.8 %copy-start.2 = (f32[64,512]{1,0:T(8,128)S(1)}, f32[64,512]{1,0:T(8,128)}, u32[]{:S(2)}) copy-start(f32[64,512]{1,0:T(8,128)} %reduce-scatter.3.cloned.1.call-done) | copy-start | bytes 393220
  189.2 43.8 %copy-start.3 = (f32[64,512]{1,0:T(8,128)S(1)}, f32[64,512]{1,0:T(8,128)}, u32[]{:S(2)}) copy-start(f32[64,512]{1,0:T(8,128)} %reduce-scatter.5.cloned.1.call-done) | copy-start | bytes 393220
Sparse Core Ops, SparseCore 0:
  101.8 19.4 reduce-scatter.2
  124.7 64.5 reduce-scatter.4
where the time goes:
time: 242 us
  blocking collectives  130 us (54%)
  waiting for transfers between devices  86.1 us (36%)
  between operations  17.8 us (7%)
  other arithmetic  4.32 us (2%)
  matrix products  3.08 us (1%)
    reduce_scatter x1, waiting for transfers between devices, on_device(): lax.psum_scatter(txt_terms.reshape(columns, img_tile.shape[1]), 'row', sc...  68 us
    psum x1, blocking collectives, on_device(): overall = lax.psum(partial_value, ('row', 'col'))  39.9 us
    all_gather x1, blocking collectives, on_device(): txt_tile = lax.all_gather(txt_own, 'row', axis=0, tiled=True)  33.2 us
    pmax x1, blocking collectives, on_device(): col_peak = lax.pmax(col_peak.reshape(-1), 'row')  21.5 us
    reduce_scatter x1, waiting for transfers between devices, on_device(): lax.psum_scatter(img_terms, 'col', scatter_dimension=0, tiled=True)  18 us
    psum x1, blocking collectives, on_device(): col_sum = lax.psum(col_sum.reshape(-1), 'row')  17.1 us
    pmax x1, blocking collectives, on_device(): row_peak = lax.pmax(row_peak, 'col')  7.09 us
    psum x1, blocking collectives, on_device(): row_sum = lax.psum(row_sum, 'col')  5.91 us
  transfers between devices with their start and end apart: 2, of which 2 were waited for; matrix products, arithmetic and copies ran while one was open for 1% of the time, Pallas kernels for 0%

commit v1 on v0

--- a/solution.py
+++ b/solution.py
@@ -2,6 +2,23 @@
 import jax.numpy as jnp
 from jax import lax
 from jax.sharding import PartitionSpec as P
+from jax.lax import axis_index, axis_size, ppermute
+
+
+def push_ladders(in_array):
+    cores_n = axis_size("row")
+    views = []
+    for c in range(1, cores_n):
+        views.append((c - 1, c))
+    big = views + [(cores_n - 1, 0)]
+    w_next = in_array
+    series = [w_next]
+    for _ in range(cores_n - 1):
+        w_next = ppermute(w_next, axis_name="row", perm=big)
+        series += [w_next]
+    kept_arr = jnp.concatenate([*reversed(series)], 0)
+    val2 = jnp.roll(kept_arr, (axis_index("row") + 1) * w_next.shape[0], 0)
+    return val2
 
 
 def normalize(embedding):
@@ -21,7 +38,7 @@
     img_own = unit_image.astype(jnp.bfloat16)
     txt_own = unit_text.astype(jnp.bfloat16)
     img_tile = lax.all_gather(img_own, "col", axis=0, tiled=True)
-    txt_tile = lax.all_gather(txt_own, "row", axis=0, tiled=True)
+    txt_tile = push_ladders(txt_own)
     columns = txt_tile.shape[0]
     block_cols = min(512, columns)
     block_count = columns // block_cols

time: 242 us -> 253 us (1.045)
  waiting for transfers between devices: 86.1 us -> 127 us
  blocking collectives: 130 us -> 97 us
  starting transfers between devices: 0.08 us -> 3.14 us
    ppermute x0 -> x7, waiting for transfers between devices: none -> 40.4 us  [push_ladders(): w_next = ppermute(w_next, axis_name='row', perm=big)]
    all_gather x1 -> x0, blocking collectives: 33.2 us -> none  [on_device(): txt_tile = lax.all_gather(txt_own, 'row', axis=0, tiled=True)]
    ppermute x0 -> x7, starting transfers between devices: none -> 3.06 us  [push_ladders(): w_next = ppermute(w_next, axis_name='row', perm=big)]
  transfers between devices with their start and end apart: 2 -> 9, of which waited for: 2 -> 9; matrix products, arithmetic and copies ran while one was open for 1% -> 1% of each run, Pallas kernels for 0% -> 0%
where the time goes in v1:
time: 253 us; the launch traced here: 252 us
  waiting for transfers between devices  127 us (50%)
  blocking collectives  97 us (38%)
  between operations  18 us (7%)
  other arithmetic  4.49 us (2%)
  starting transfers between devices  3.14 us (1%)
  matrix products  3.09 us (1%)
    reduce_scatter x1, waiting for transfers between devices, on_device(): lax.psum_scatter(txt_terms.reshape(columns, img_tile.shape[1]), 'row', sc...  68 us
    ppermute x7, waiting for transfers between devices, push_ladders(): w_next = ppermute(w_next, axis_name='row', perm=big)  40.4 us
    psum x1, blocking collectives, on_device(): overall = lax.psum(partial_value, ('row', 'col'))  39.9 us
    pmax x1, blocking collectives, on_device(): col_peak = lax.pmax(col_peak.reshape(-1), 'row')  21.8 us
    reduce_scatter x1, waiting for transfers between devices, on_device(): lax.psum_scatter(img_terms, 'col', scatter_dimension=0, tiled=True)  18.1 us
    psum x1, blocking collectives, on_device(): col_sum = lax.psum(col_sum.reshape(-1), 'row')  17.1 us
    pmax x1, blocking collectives, on_device(): row_peak = lax.pmax(row_peak, 'col')  6.23 us
    all_gather x1, blocking collectives, on_device(): img_tile = lax.all_gather(img_own, 'col', axis=0, tiled=True)  6.05 us
  transfers between devices with their start and end apart: 9, of which 9 were waited for; matrix products, arithmetic and copies ran while one was open for 1% of the time, Pallas kernels for 0%

profile of v1, /device:TPU:0, one launch (start us, length us, event | category | flops | bytes accessed | tf_op | source)
XLA Modules:
  0.0 252.4 jit_solution(3557928599187487725)
XLA Ops:
  7.2 0.0 copy-start
  7.2 0.0 reduce-scatter.3.cloned.1.call-start
  7.2 1.0 fusion.3
  8.2 0.0 copy-done
  8.2 0.0 copy-start.1
  8.2 0.1 fusion.10
  8.3 3.0 %collective-permute-start = (bf16[64,512]{1,0:T(8,128)(2,1)S(1)}, bf16[64,512]{1,0:T(8,128)(2,1)S(1)}, u32[]{:S(2)}, u32[]{:S(2)}) collective-permute-start(bf16[64,512]{1,0:T(8,128)(2,1)S(1)} %fusion.10), channel_id=1, source_target_pairs={{0,4},{4,8},{8,12},{12,16},{16,20},{20,24},{24,28},{28,0},{1,5},{5... | collective-permute-start | bytes 196616 | tf_op jit(solution)/shard_map/ppermute | solution.py:17
  11.4 5.3 %collective-permute-done = bf16[64,512]{1,0:T(8,128)(2,1)S(1)} collective-permute-done((bf16[64,512]{1,0:T(8,128)(2,1)S(1)}, bf16[64,512]{1,0:T(8,128)(2,1)S(1)}, u32[]{:S(2)}, u32[]{:S(2)}) %collective-permute-start) | collective-permute-done | bytes 65568 | tf_op jit(solution)/shard_map/ppermute | solution.py:17
  16.7 0.0 collective-permute-start.1
  16.7 7.0 %collective-permute-done.1 = bf16[64,512]{1,0:T(8,128)(2,1)S(1)} collective-permute-done((bf16[64,512]{1,0:T(8,128)(2,1)S(1)}, bf16[64,512]{1,0:T(8,128)(2,1)S(1)}, u32[]{:S(2)}, u32[]{:S(2)}) %collective-permute-start.1) | collective-permute-done | bytes 65568 | tf_op jit(solution)/shard_map/ppermute | solution.py:17
  23.6 0.0 collective-permute-start.2
  23.6 7.0 %collective-permute-done.2 = bf16[64,512]{1,0:T(8,128)(2,1)S(1)} collective-permute-done((bf16[64,512]{1,0:T(8,128)(2,1)S(1)}, bf16[64,512]{1,0:T(8,128)(2,1)S(1)}, u32[]{:S(2)}, u32[]{:S(2)}) %collective-permute-start.2) | collective-permute-done | bytes 65568 | tf_op jit(solution)/shard_map/ppermute | solution.py:17
  30.6 0.0 collective-permute-start.3
  30.6 0.0 copy-done.1
  30.6 0.1 fusion.2
  30.7 6.8 %collective-permute-done.3 = bf16[64,512]{1,0:T(8,128)(2,1)S(1)} collective-permute-done((bf16[64,512]{1,0:T(8,128)(2,1)S(1)}, bf16[64,512]{1,0:T(8,128)(2,1)S(1)}, u32[]{:S(2)}, u32[]{:S(2)}) %collective-permute-start.3) | collective-permute-done | bytes 65568 | tf_op jit(solution)/shard_map/ppermute | solution.py:17
  37.5 0.0 collective-permute-start.4
  37.6 7.3 %collective-permute-done.4 = bf16[64,512]{1,0:T(8,128)(2,1)S(1)} collective-permute-done((bf16[64,512]{1,0:T(8,128)(2,1)S(1)}, bf16[64,512]{1,0:T(8,128)(2,1)S(1)}, u32[]{:S(2)}, u32[]{:S(2)}) %collective-permute-start.4) | collective-permute-done | bytes 65568 | tf_op jit(solution)/shard_map/ppermute | solution.py:17
  44.8 0.0 collective-permute-start.5
  44.8 0.1 fusion.9
  45.6 6.2 %collective-permute-done.5 = bf16[64,512]{1,0:T(8,128)(2,1)S(1)} collective-permute-done((bf16[64,512]{1,0:T(8,128)(2,1)S(1)}, bf16[64,512]{1,0:T(8,128)(2,1)S(1)}, u32[]{:S(2)}, u32[]{:S(2)}) %collective-permute-start.5) | collective-permute-done | bytes 65568 | tf_op jit(solution)/shard_map/ppermute | solution.py:17
  51.8 0.0 collective-permute-start.6
  51.8 6.0 %all_gather.3 = bf16[256,512]{1,0:T(8,128)(2,1)S(1)} all-gather(bf16[64,512]{1,0:T(8,128)(2,1)S(1)} %fusion.9), channel_id=1, replica_groups=mesh['row'=8,'col'=4] {'col'}, dimensions={0}, use_global_device_ids=true | all-gather | bytes 327680 | tf_op jit(solution)/shard_map/all_gather | solution.py:40
  57.9 0.9 collective-permute-done.6
  58.9 0.1 constant_dynamic-update-slice_fusion.8
  59.1 0.1 constant_dynamic-update-slice_fusion
  59.1 0.4 fusion.11
  59.6 6.2 %pmax.14 = f32[256]{0:T(256)S(1)} all-reduce(f32[256]{0:T(256)S(1)} %broadcast_maximum_fusion), channel_id=1, replica_groups=mesh['row'=8,'col'=4] {'col'}, use_global_device_ids=true, to_apply=%region_3.4 | all-reduce | flops 256 | bytes 2048 | tf_op jit(solution)/shard_map/pmax | solution.py:59
  65.8 21.8 %pmax.15 = f32[512]{0:T(512)S(1)} all-reduce(f32[512]{0:T(512)S(1)} %get-tuple-element.47), channel_id=1, replica_groups=mesh['row'=8,'col'=4] {'row'}, use_global_device_ids=true, to_apply=%region_9.10 | all-reduce | flops 512 | bytes 4096 | tf_op jit(solution)/shard_map/pmax | solution.py:60
  87.6 0.2 exponential_reduce_fusion
  87.9 5.9 %psum.21 = f32[256]{0:T(256)S(1)} all-reduce(f32[256]{0:T(256)S(1)} %get-tuple-element.46), channel_id=1, replica_groups=mesh['row'=8,'col'=4] {'col'}, use_global_device_ids=true, to_apply=%region_5.6 | all-reduce | flops 256 | bytes 2048 | tf_op jit(solution)/shard_map/psum | solution.py:71
  93.8 17.1 %psum.22 = f32[512]{0:T(512)S(1)} all-reduce(f32[512]{0:T(512)S(1)} %get-tuple-element.45), channel_id=1, replica_groups=mesh['row'=8,'col'=4] {'row'}, use_global_device_ids=true, to_apply=%region_11.12 | all-reduce | flops 512 | bytes 4096 | tf_op jit(solution)/shard_map/psum | solution.py:72
  110.9 1.2 convolution_multiply_fusion.1
  112.1 0.0 reduce-scatter.3.cloned.1.call-update
  112.1 0.0 reduce-scatter.5.cloned.1.call-start
  112.2 1.5 convolution_multiply_fusion
  113.6 0.0 reduce-scatter.5.cloned.1.call-update
  113.6 18.1 %reduce-scatter.3.cloned.1.call-done = f32[64,512]{1,0:T(8,128)} async-done(((f32[256,512]{1,0:T(8,128)}), f32[64,512]{1,0:T(8,128)}) %reduce-scatter.3.cloned.1.call-update) | async-done | bytes 131088 | tf_op jit(solution)/shard_map/reduce_scatter | solution.py:111
  131.7 68.0 %reduce-scatter.5.cloned.1.call-done = f32[64,512]{1,0:T(8,128)} async-done(((f32[512,512]{1,0:T(8,128)}), f32[64,512]{1,0:T(8,128)}) %reduce-scatter.5.cloned.1.call-update) | async-done | bytes 131088 | tf_op jit(solution)/shard_map/reduce_scatter | solution.py:108
  199.7 0.0 copy-start.2
  199.7 0.0 copy-start.3
  199.7 1.3 multiply_reduce_fusion
  201.0 0.7 subtract_reduce_fusion
  203.0 39.9 %psum.23 = f32[]{:T(128)} all-reduce(f32[]{:T(128)S(6)} %add.77), channel_id=1, replica_groups=mesh['row'=8,'col'=4] {'row','col'}, use_global_device_ids=true, to_apply=%region_13.14 | all-reduce | flops 1 | bytes 8 | tf_op jit(solution)/shard_map/psum | solution.py:82
  243.5 0.0 copy-done.2
  243.5 0.0 copy-done.3
  243.5 0.8 subtract_divide_fusion
  (19 shorter events, 0.1 us)
Async XLA Ops:
  7.2 1.0 copy-start
  7.2 124.5 %reduce-scatter.3.cloned.1.call-start = ((), (), s32[]{:S(2)}) async-start(), calls=%async_computation.2 | async-start | bytes 655360 | tf_op jit(solution)/shard_map/reduce_scatter | solution.py:111
  8.2 22.4 %copy-start.1 = (bf16[64,512]{1,0:T(8,128)(2,1)S(1)}, bf16[64,512]{1,0:T(8,128)(2,1)}, u32[]{:S(2)}) copy-start(bf16[64,512]{1,0:T(8,128)(2,1)} %param.3) | copy-start | bytes 196612
  8.3 8.3 %collective-permute-start = (bf16[64,512]{1,0:T(8,128)(2,1)S(1)}, bf16[64,512]{1,0:T(8,128)(2,1)S(1)}, u32[]{:S(2)}, u32[]{:S(2)}) collective-permute-start(bf16[64,512]{1,0:T(8,128)(2,1)S(1)} %fusion.10), channel_id=1, source_target_pairs={{0,4},{4,8},{8,12},{12,16},{16,20},{20,24},{24,28},{28,0},{1,5},{5... | collective-permute-start | bytes 196616 | tf_op jit(solution)/shard_map/ppermute | solution.py:17
  16.7 7.0 %collective-permute-start.1 = (bf16[64,512]{1,0:T(8,128)(2,1)S(1)}, bf16[64,512]{1,0:T(8,128)(2,1)S(1)}, u32[]{:S(2)}, u32[]{:S(2)}) collective-permute-start(bf16[64,512]{1,0:T(8,128)(2,1)S(1)} %collective-permute-done), channel_id=1, source_target_pairs={{0,4},{4,8},{8,12},{12,16},{16,20},{20,24},{24,28},{28,0},{1,5},{5... | collective-permute-start | bytes 196616 | tf_op jit(solution)/shard_map/ppermute | solution.py:17
  23.6 7.0 %collective-permute-start.2 = (bf16[64,512]{1,0:T(8,128)(2,1)S(1)}, bf16[64,512]{1,0:T(8,128)(2,1)S(1)}, u32[]{:S(2)}, u32[]{:S(2)}) collective-permute-start(bf16[64,512]{1,0:T(8,128)(2,1)S(1)} %collective-permute-done.1), channel_id=1, source_target_pairs={{0,4},{4,8},{8,12},{12,16},{16,20},{20,24},{24,28},{28,0},{1,5},{5... | collective-permute-start | bytes 196616 | tf_op jit(solution)/shard_map/ppermute | solution.py:17
  30.6 7.0 %collective-permute-start.3 = (bf16[64,512]{1,0:T(8,128)(2,1)S(1)}, bf16[64,512]{1,0:T(8,128)(2,1)S(1)}, u32[]{:S(2)}, u32[]{:S(2)}) collective-permute-start(bf16[64,512]{1,0:T(8,128)(2,1)S(1)} %collective-permute-done.2), channel_id=1, source_target_pairs={{0,4},{4,8},{8,12},{12,16},{16,20},{20,24},{24,28},{28,0},{1,5},{5... | collective-permute-start | bytes 196616 | tf_op jit(solution)/shard_map/ppermute | solution.py:17
  37.5 7.3 %collective-permute-start.4 = (bf16[64,512]{1,0:T(8,128)(2,1)S(1)}, bf16[64,512]{1,0:T(8,128)(2,1)S(1)}, u32[]{:S(2)}, u32[]{:S(2)}) collective-permute-start(bf16[64,512]{1,0:T(8,128)(2,1)S(1)} %collective-permute-done.3), channel_id=1, source_target_pairs={{0,4},{4,8},{8,12},{12,16},{16,20},{20,24},{24,28},{28,0},{1,5},{5... | collective-permute-start | bytes 196616 | tf_op jit(solution)/shard_map/ppermute | solution.py:17
  44.8 7.0 %collective-permute-start.5 = (bf16[64,512]{1,0:T(8,128)(2,1)S(1)}, bf16[64,512]{1,0:T(8,128)(2,1)S(1)}, u32[]{:S(2)}, u32[]{:S(2)}) collective-permute-start(bf16[64,512]{1,0:T(8,128)(2,1)S(1)} %collective-permute-done.4), channel_id=1, source_target_pairs={{0,4},{4,8},{8,12},{12,16},{16,20},{20,24},{24,28},{28,0},{1,5},{5... | collective-permute-start | bytes 196616 | tf_op jit(solution)/shard_map/ppermute | solution.py:17
  51.8 7.0 %collective-permute-start.6 = (bf16[64,512]{1,0:T(8,128)(2,1)S(1)}, bf16[64,512]{1,0:T(8,128)(2,1)S(1)}, u32[]{:S(2)}, u32[]{:S(2)}) collective-permute-start(bf16[64,512]{1,0:T(8,128)(2,1)S(1)} %collective-permute-done.5), channel_id=1, source_target_pairs={{0,4},{4,8},{8,12},{12,16},{16,20},{20,24},{24,28},{28,0},{1,5},{5... | collective-permute-start | bytes 196616 | tf_op jit(solution)/shard_map/ppermute | solution.py:17
  112.1 87.6 %reduce-scatter.5.cloned.1.call-start = ((), (), s32[]{:S(2)}) async-start(), calls=%async_computation.3 | async-start | bytes 1179648 | tf_op jit(solution)/shard_map/reduce_scatter | solution.py:108
  199.7 43.8 %copy-start.2 = (f32[64,512]{1,0:T(8,128)S(1)}, f32[64,512]{1,0:T(8,128)}, u32[]{:S(2)}) copy-start(f32[64,512]{1,0:T(8,128)} %reduce-scatter.3.cloned.1.call-done) | copy-start | bytes 393220
  199.7 43.8 %copy-start.3 = (f32[64,512]{1,0:T(8,128)S(1)}, f32[64,512]{1,0:T(8,128)}, u32[]{:S(2)}) copy-start(f32[64,512]{1,0:T(8,128)} %reduce-scatter.5.cloned.1.call-done) | copy-start | bytes 393220
Sparse Core Ops, SparseCore 0:
  112.2 19.4 reduce-scatter.2
  135.1 64.5 reduce-scatter.4
